TPU v7x, 256 devices: a whole 4x4x8 slice. The times are simulated.
256 devices in a mesh: slab: 32 (over z, x_lo, core), blk: 8 (over x_hi, y).
Axes of the slice: x: 4 (x_hi: 2, x_lo: 2; x = x_hi * 2 + x_lo), y: 4, z: 8, core: 2. Of those that a mesh axis runs over, the one named last changes fastest.
Arguments:
- modes: bfloat16 [131072, 2048], P('slab', 'blk'), may hold values from -6 to 6
- stiffness: bfloat16 [131072, 512], P('slab'), may hold values from -0.0007324219 to 0.0007324219
- offsets: int32 [2048, 8], P('slab'), may hold values from -4 to 4, as said below
Outputs:
- reduced: float32 [2048, 2048], P('blk', 'slab')
Inputs may be any that keep to these rules, and one draw needn't show every extreme that they name: Each row of offsets lists 8 different values, in an order drawn from the seed: all of -4 to 4 except one nonzero value of magnitude below 4.
All inputs are finite; a program needn't handle non-finite values.
Results may differ from a plain program's by a relative error of at most 0.0029.
Values may be sent and summed in bfloat16 or wider, within the bound.
A program may use at most 128 MiB of HBM per device.

v0:
```python
import jax
import jax.numpy as jnp
from jax import lax
from jax.sharding import PartitionSpec as P

M = 2048
BS = 64
HB = 4
BPR = 8


def padded_2(cells, sides, width):
    for axis, dim in sides:
        count = lax.axis_size(axis)
        ends = count - 1
        head = lax.slice_in_dim(cells, 0, width, axis=dim)
        tail = lax.slice_in_dim(cells, cells.shape[dim] - width, cells.shape[dim], axis=dim)
        cells = jnp.concatenate(
            [
                lax.ppermute(tail, axis, [(i, (i + 1) % count) for i in range(ends)]),
                cells,
                lax.ppermute(head, axis, [((i + 1) % count, i) for i in range(ends)]),
            ],
            axis=dim,
        )
    return cells


def apply_stiffness(modes, stiffness, offsets):
    rows, panel = modes.shape
    nblocks = rows // BS
    padded = padded_2(modes, (("slab", 0),), HB * BS)
    blocks = padded.reshape(nblocks + 2 * HB, BS, panel)
    kblocks = stiffness.reshape(nblocks, BS, BPR, BS)
    base = jnp.arange(nblocks, dtype=jnp.int32)
    total = jnp.zeros((nblocks, BS, panel), jnp.float32)
    for column in range(BPR):
        where = base + offsets[:, column] + HB
        picked = jnp.take(blocks, where, axis=0)
        total = total + jnp.einsum(
            "nab,nbm->nam", kblocks[:, :, column, :], picked, preferred_element_type=jnp.float32
        )
    return total.reshape(rows, panel).astype(jnp.bfloat16)


def body(modes, stiffness, offsets):
    kphi = apply_stiffness(modes, stiffness, offsets)
    slabs = lax.axis_size("slab")
    width = M // slabs
    partial_rows = lax.dot_general(
        modes,
        lax.all_gather(kphi, "blk", axis=1, tiled=True),
        (((0,), (0,)), ((), ())),
        preferred_element_type=jnp.float32,
    )
    summed = lax.psum(partial_rows, "slab")
    start_col = lax.axis_index("slab") * width
    return lax.dynamic_slice_in_dim(summed, start_col, width, 1)


def solution(mesh):
    in_specs = (P("slab", "blk"), P("slab", None), P("slab", None))
    out_specs = P("blk", "slab")
    return jax.shard_map(body, mesh=mesh, in_specs=in_specs, out_specs=out_specs, check_vma=False)
```

profile of v0, /device:TPU:19, one launch (start us, length us, event | category | flops | bytes accessed | tf_op | source)
XLA Modules:
  0.0 562.7 jit_solution(14597614956319123974)
XLA Ops:
  6.5 0.0 all-gather.2.cloned.1.call-start
  6.5 1.0 fusion.40
  7.5 4.1 collective-permute-start
  11.6 1.9 collective-permute-start.1
  13.5 1.0 compare_and_fusion
  14.5 11.2 %reshape.14 = bf16[64,64,8,64]{3,2,1,0:T(8,128)(2,1)} reshape(bf16[4096,512]{1,0:T(8,128)(2,1)} %param.6) | data formatting | bytes 8388608 | tf_op jit(solution)/shard_map/reshape | solution.py:34
  25.8 40.3 %fusion.39 = (bf16[64,64,1,64]{3,2,1,0:T(2,128)(2,1)}, bf16[64,64,1,64]{3,2,1,0:T(2,128)(2,1)}, bf16[64,64,1,64]{3,2,1,0:T(2,128)(2,1)}, bf16[64,64,1,64]{3,2,1,...) fusion(bf16[64,64,8,64]{3,2,1,0:T(8,128)(2,1)} %reshape.14), kind=kLoop, calls=%fused_computation.91 | loop fusion | bytes 8388608 | tf_op jit(solution)/shard_map/slice | solution.py:41
  66.2 0.0 collective-permute-done
  66.2 0.0 collective-permute-done.1
  66.2 0.0 copy-done.13
  66.2 0.2 pad_maximum_fusion
  66.4 2.0 gather_fusion.1
  68.3 2.0 gather_fusion
  70.3 2.1 gather_fusion.5
  72.4 2.0 gather_fusion.4
  74.5 2.0 gather_fusion.3
  76.5 2.0 gather_fusion.2
  78.4 2.1 gather_fusion.6
  80.5 2.1 gather_fusion.7
  82.6 3.1 fusion.11
  85.7 0.0 copy-done.6
  85.8 0.3 copy-done.12
  86.1 0.8 fusion.13
  86.9 0.8 copy-done.5
  87.7 0.6 copy-done.11
  88.3 2.7 fusion.3
  91.0 0.0 copy-done.4
  91.0 0.6 copy-done.10
  91.7 2.8 fusion.5
  94.5 0.0 copy-done.3
  94.5 0.6 copy-done.9
  95.1 2.7 fusion.7
  97.8 0.0 copy-done.2
  97.8 0.6 copy-done.8
  98.4 2.7 fusion.9
  101.2 0.0 copy-done.1
  101.2 0.6 copy-done.7
  101.8 2.7 fusion.1
  104.6 0.0 copy-done
  104.6 10.3 %add_convert_fusion = bf16[64,256,64]{1,2,0:T(8,128)(2,1)} fusion(f32[64,256,64]{1,2,0:T(8,128)} %fusion.1, f32[64,256,64]{1,2,0:T(8,128)} %fusion.3, f32[64,256,64]{1,2,0:T(8,128)} %fusion.5, f32[64,256,64]{1,2,0:T(8,128)} %fusion.7, f32[64,256,64]{1,2,0:T(8,128)} %fusion.9, f32[64,256,64]{1,2,0:T(8,128)S(1)} %fusion.13, f32[64,256,64]{1,2,0:T(8,128)S(1)} %fusion.11, ...), kind=kOutput, calls=%fused_computation.8 | convolution fusion | flops 143654912 | bytes 34078784 | tf_op jit(solution)/shard_map/nab,nbm->nam/dot_general | solution.py:40
  114.9 0.0 all-gather.2.cloned.1.call-update
  114.9 0.0 all-reduce.2.cloned.1.call-start
  115.0 198.8 %all-gather.2.cloned.1.call-done = bf16[4096,2048]{1,0:T(8,128)(2,1)} async-done(((bf16[4096,256]{1,0:T(8,128)(2,1)}), bf16[4096,2048]{1,0:T(8,128)(2,1)}) %all-gather.2.cloned.1.call-update) | async-done | bytes 16777232 | tf_op jit(solution)/shard_map/all_gather | solution.py:52
  313.8 0.0 copy-done.14
  313.8 9.7 %convolution_bitcast_fusion = f32[256,2048]{0,1:T(8,128)} fusion(bf16[4096,2048]{1,0:T(8,128)(2,1)} %all-gather.2.cloned.1.call-done, bf16[4096,256]{1,0:T(8,128)(2,1)S(1)} %copy-done.14), kind=kOutput, calls=%fused_computation.9 | convolution fusion | flops 4294967296 | bytes 20971520 | tf_op jit(solution)/shard_map/dot_general | solution.py:50
  323.5 0.0 all-reduce.2.cloned.1.call-update
  323.5 230.9 %all-reduce.2.cloned.1.call-done = f32[256,2048]{0,1:T(8,128)} async-done(((f32[256,2048]{0,1:T(8,128)}), f32[256,2048]{0,1:T(8,128)}) %all-reduce.2.cloned.1.call-update) | async-done | bytes 2097168 | tf_op jit(solution)/shard_map/psum | solution.py:56
  554.4 1.5 constant_dynamic-slice_fusion
  (19 shorter events, 0.0 us)
Async XLA Ops:
  6.5 307.2 %all-gather.2.cloned.1.call-start = ((), (), s32[]{:S(2)}) async-start(), calls=%async_computation | async-start | bytes 18874368 | tf_op jit(solution)/shard_map/all_gather | solution.py:52
  7.5 58.6 %collective-permute-start = (bf16[256,256]{1,0:T(8,128)(2,1)S(1)}, bf16[256,256]{1,0:T(8,128)(2,1)S(1)}, u32[]{:S(2)}, u32[]{:S(2)}) collective-permute-start(bf16[256,256]{1,0:T(8,128)(2,1)S(1)} %get-tuple-element.30), channel_id=1, source_target_pairs={{0,8},{8,16},{16,24},{24,32},{32,40},{40,48},{48,56},{56,64},{64,7... | collective-permute-start | bytes 393224 | tf_op jit(solution)/shard_map/ppermute | solution.py:20
  11.6 54.6 %collective-permute-start.1 = (bf16[256,256]{1,0:T(8,128)(2,1)S(1)}, bf16[256,256]{1,0:T(8,128)(2,1)S(1)}, u32[]{:S(2)}, u32[]{:S(2)}) collective-permute-start(bf16[256,256]{1,0:T(8,128)(2,1)S(1)} %get-tuple-element.31), channel_id=1, source_target_pairs={{8,0},{16,8},{24,16},{32,24},{40,32},{48,40},{56,48},{64,56},{72,6... | collective-permute-start | bytes 393224 | tf_op jit(solution)/shard_map/ppermute | solution.py:22
  25.8 40.4 %copy-start.13 = (bf16[4096,256]{1,0:T(8,128)(2,1)S(1)}, bf16[4096,256]{1,0:T(8,128)(2,1)}, u32[]{:S(2)}) copy-start(bf16[4096,256]{1,0:T(8,128)(2,1)} %param.5) | copy-start | bytes 6291460
  82.6 3.2 copy-start.6
  82.6 3.5 copy-start.12
  86.1 1.6 copy-start.5
  86.1 2.2 copy-start.11
  88.3 2.8 copy-start.4
  88.3 3.4 copy-start.10
  91.7 2.8 copy-start.3
  91.7 3.4 copy-start.9
  95.1 2.8 copy-start.2
  95.1 3.4 copy-start.8
  98.4 2.8 copy-start.1
  98.4 3.4 copy-start.7
  101.8 2.7 copy-start
  114.9 198.9 %copy-start.14 = (bf16[4096,256]{1,0:T(8,128)(2,1)S(1)}, bf16[4096,256]{1,0:T(8,128)(2,1)}, u32[]{:S(2)}) copy-start(bf16[4096,256]{1,0:T(8,128)(2,1)} %param.5) | copy-start | bytes 6291460
  114.9 439.5 %all-reduce.2.cloned.1.call-start = ((), (), s32[]{:S(2)}) async-start(), calls=%async_computation.1 | async-start | bytes 4194304 | tf_op jit(solution)/shard_map/psum | solution.py:56
Sparse Core Ops, SparseCore 0:
  115.0 198.6 all-gather.1
  323.6 230.7 all-reduce.1
where the time goes:
time: 568 us; the launch traced here: 563 us
  waiting for transfers between devices  430 us (76%)
  local copies, waits for them, and re-layouts  74.5 us (13%)
  matrix products  37.7 us (7%)
  between operations  13.5 us (2%)
  starting transfers between devices  6.04 us (1%)
    psum x1, waiting for transfers between devices, body(): summed = lax.psum(partial_rows, 'slab')  231 us
    all_gather x1, waiting for transfers between devices, body(): lax.all_gather(kphi, 'blk', axis=1, tiled=True)  199 us
    slice x1, local copies, waits for them, and re-layouts, apply_stiffness(): kblocks[:, :, column, :]  40.3 us
    dot_general x8, matrix products, apply_stiffness(): jnp.einsum('nab,nbm->nam', kblocks[:, :, column, :], picked, preferred_el...  28 us
    gather x8, local copies, waits for them, and re-layouts, apply_stiffness(): picked = jnp.take(blocks, where, axis=0)  16.2 us
  transfers between devices with their start and end apart: 4, of which 2 were waited for; matrix products, arithmetic and copies ran while one was open for 9% of the time, Pallas kernels for 0%

commit v1 on v0

v1 whole, which is shorter than its diff:
```python
import jax
import jax.numpy as jnp
from jax import lax
from jax.experimental import pallas as pl
from jax.experimental.pallas import tpu as pltpu
from jax.sharding import PartitionSpec as P

MESH = pl.DeviceIdType.MESH
BS = 64
CH = 256
BPC = CH // BS
W = 256
F32 = jnp.float32
BF16 = jnp.bfloat16

O, U, D, Q = (0, 0), (0, 1), (0, 3), (1, 1)
PAIRS = ((O, O), (O, Q), (U, O), (U, Q), (D, O), (D, Q), (D, U), (Q, O))


def kernel(
    modes, stiff, offs, out,
    own, kv, up, dn, qp, halo, ring, kphi, acc, xr, sb, fr,
    lsem, yu_s, yu_r, yd_s, yd_r, xq_s, xq_r, h_s, h_r, c_s, c_r, f_s, f_r,
):
    s, b = lax.axis_index("slab"), lax.axis_index("blk")
    z, xl, core = s // 4, (s // 2) % 2, s % 2
    xh, y = b // 4, b % 4
    nch = modes.shape[0] // CH
    slabs = lax.axis_size("slab")

    def blk_at(d):
        return ((xh + d[0]) % 2) * 4 + (y + d[1]) % 4

    outer = lax.rem(s + 2 * core - 1 + slabs, slabs)
    inner = s + 1 - 2 * core
    y_up, y_dn, x_far = (s, blk_at((0, 1))), (s, blk_at((0, 3))), (s, blk_at((1, 0)))
    across, beyond = (inner, b), (outer, b)

    def chunk(t):
        return t * core + (nch - 1 - t) * (1 - core)

    def rows(t):
        return pl.ds(pl.multiple_of(chunk(t) * CH, CH), CH)

    way = 2 * core - 1

    def site_of():
        dx, dy = (z // 4 + xh) % 2, (z % 4 + 4 - y) % 4
        bx, by = jnp.int32(0), jnp.int32(0)
        for r, c in PAIRS:
            hit = jnp.logical_and(dx == (c[0] - r[0]) % 2, dy == (c[1] - r[1]) % 4).astype(jnp.int32)
            bx = bx + hit * ((xh + r[0]) % 2)
            by = by + hit * ((y + 4 - r[1]) % 4)
        return bx * 4 + by

    site = site_of()
    mine = z * 2 + xl
    to_self = (site == b).astype(jnp.int32)

    copy_k = pltpu.make_async_copy(stiff, kv, lsem.at[0])
    copy_o = pltpu.make_async_copy(modes, own, lsem.at[1])
    copy_k.start()
    copy_o.start()

    barrier = pltpu.get_barrier_semaphore()
    for dev in (y_up, y_dn, x_far, across, beyond):
        pl.semaphore_signal(barrier, inc=1, device_id=dev, device_id_type=MESH)

    @pl.loop(0, 16)
    def _(i):
        @pl.when(jnp.logical_or(to_self == 0, i != mine))
        def _():
            pl.semaphore_signal(barrier, inc=1, device_id=(i * 2 + core, site), device_id_type=MESH)

    pl.semaphore_wait(barrier, 5 + 16 - to_self)

    def remote(src, dst, ssem, rsem, dev):
        return pltpu.make_async_remote_copy(src, dst, ssem, rsem, device_id=dev, device_id_type=MESH)

    def send_u(t):
        return remote(modes.at[rows(t)], up.at[rows(t)], yu_s.at[t], yu_r.at[t], y_dn)

    def send_d(t):
        return remote(modes.at[rows(t)], dn.at[rows(t)], yd_s.at[t], yd_r.at[t], y_up)

    def send_q(t):
        return remote(up.at[rows(t)], qp.at[rows(t)], xq_s.at[t], xq_r.at[t], x_far)

    ho_out = remote(modes.at[rows(nch - 1)], halo.at[0, 1], h_s.at[0], h_r.at[0], beyond)
    ho_in = remote(modes.at[rows(0)], halo.at[0, 0], h_s.at[1], h_r.at[1], across)
    hu_out = remote(halo.at[0, 1], halo.at[2, 1], h_s.at[2], h_r.at[2], y_dn)
    hu_in = remote(up.at[rows(0)], halo.at[2, 0], h_s.at[3], h_r.at[3], across)
    hq_out = remote(halo.at[2, 1], halo.at[1, 1], h_s.at[4], h_r.at[4], x_far)
    hq_in = remote(qp.at[rows(0)], halo.at[1, 0], h_s.at[5], h_r.at[5], across)

    ho_out.start()
    ho_in.start()

    @pl.loop(0, nch)
    def _(t):
        send_u(t).start()
        send_d(t).start()

    acc[...] = jnp.zeros_like(acc)
    copy_k.wait()
    copy_o.wait()
    ho_out.wait_recv()
    hu_out.start()

    def fill(slot, parts):
        for p, part in enumerate(parts):
            ring[pl.ds(slot * BPC, BPC), :, p * W:(p + 1) * W] = part.reshape(BPC, BS, W)

    def compute(j):
        c = chunk(j)
        for i in range(BPC):
            line = c * BPC + i
            where = []
            for col in range(8):
                pos = offs[line, col] + i
                slot = (j + 1 + way * (pos >> 2)) & 3
                where.append(slot * BPC + (pos & 3))
            lhs = kv[pl.ds(pl.multiple_of(line * BS, BS), BS), :]
            for p in range(3):
                gathered = jnp.concatenate([ring[w, :, p * W:(p + 1) * W] for w in where], axis=0)
                kphi[i * BS:(i + 1) * BS, p * W:(p + 1) * W] = jnp.dot(
                    lhs, gathered, preferred_element_type=F32
                ).astype(BF16)
        first = 0
        for ref, n in ((own, 2), (up, 2), (dn, 3), (qp, 1)):
            prod = lax.dot_general(
                kphi[:, : n * W], ref[rows(j), :], (((0,), (0,)), ((), ())), preferred_element_type=F32
            )
            acc[first:first + n] += prod.reshape(n, 2, 2, BS, W)
            first += n

    lag = 2

    @pl.loop(0, nch + lag + 1)
    def _(t):
        @pl.when(t < nch)
        def _():
            send_u(t).wait_recv()
            send_q(t).start()

        @pl.when(t == 0)
        def _():
            hu_in.start()

        @pl.when(t == 2)
        def _():
            hu_out.wait_recv()
            hq_out.start()

        j = t - lag

        @pl.when(j == 0)
        def _():
            send_q(0).wait_recv()
            hq_in.start()
            hu_in.wait_recv()
            ho_in.wait_recv()
            hq_in.wait_recv()
            fill(0, (halo[0, 0], halo[1, 0], halo[2, 0]))

        @pl.when(jnp.logical_and(j >= 0, j < nch))
        def _():
            @pl.when(j > 0)
            def _():
                send_q(j).wait_recv()

            fill((j + 1) & 3, (own[rows(j), :], qp[rows(j), :], up[rows(j), :]))

        @pl.when(j == nch)
        def _():
            hq_out.wait_recv()
            inside = jnp.logical_and(s + core > 0, s + core < slabs).astype(F32)
            fill(
                (nch + 1) & 3,
                [jnp.where(inside > 0, halo[p, 1], jnp.zeros((CH, W), BF16)) for p in range(3)],
            )

        @pl.when(j >= 1)
        def _():
            send_d(j - 1).wait_recv()
            compute(j - 1)

    def swap(p):
        return remote(acc.at[p, :, 1 - core], xr.at[p], c_s.at[p], c_r.at[p], across)

    for p in range(8):
        swap(p).start()

    def final(p, h):
        r, c = PAIRS[p]
        dev = ((((xh + c[0]) % 2) * 4 + (y + c[1]) % 4) * 4 + h * 2 + core, blk_at(r))
        return remote(sb.at[p, h], fr.at[mine], f_s.at[p, h], f_r.at[mine], dev), dev

    def is_self(p, h, dev):
        return jnp.logical_and(dev[0] == s, dev[1] == b)

    for p in range(8):
        swap(p).wait_recv()
        sb[p] = (acc[p, :, core] + xr[p]).astype(BF16)
        for h in range(2):
            cp, dev = final(p, h)
            if PAIRS[p][0] == O:
                @pl.when(is_self(p, h, dev))
                def _():
                    fr[mine] = sb[p, h]

                @pl.when(jnp.logical_not(is_self(p, h, dev)))
                def _():
                    cp.start()
            else:
                cp.start()

    total = jnp.zeros((BS, W), F32)
    out[...] = total

    @pl.loop(0, 16)
    def _(i):
        @pl.when(jnp.logical_or(to_self == 0, i != mine))
        def _():
            remote(sb.at[0, 0], fr.at[i], f_s.at[0, 0], f_r.at[i], across).wait_recv()

        out[...] += fr[i].astype(F32)

    for cp in (ho_out, ho_in, hu_out, hu_in, hq_out, hq_in):
        cp.wait_send()

    @pl.loop(0, nch)
    def _(t):
        send_u(t).wait_send()
        send_d(t).wait_send()
        send_q(t).wait_send()

    for p in range(8):
        swap(p).wait_send()
        for h in range(2):
            cp, dev = final(p, h)
            if PAIRS[p][0] == O:
                @pl.when(jnp.logical_not(is_self(p, h, dev)))
                def _():
                    cp.wait_send()
            else:
                cp.wait_send()


def body(modes, stiffness, offsets):
    n, w = modes.shape
    nch = n // CH
    dma = pltpu.SemaphoreType.DMA
    res = pl.pallas_call(
        kernel,
        out_shape=jax.ShapeDtypeStruct((BS, W), F32),
        in_specs=[
            pl.BlockSpec(memory_space=pl.ANY),
            pl.BlockSpec(memory_space=pl.ANY),
            pl.BlockSpec(memory_space=pltpu.SMEM),
        ],
        out_specs=pl.BlockSpec(memory_space=pltpu.VMEM),
        scratch_shapes=[
            pltpu.VMEM((n, w), BF16),
            pltpu.VMEM((n, 8 * BS), BF16),
            pltpu.VMEM((n, w), BF16),
            pltpu.VMEM((n, w), BF16),
            pltpu.VMEM((n, w), BF16),
            pltpu.VMEM((3, 2, CH, w), BF16),
            pltpu.VMEM((4 * BPC, BS, 3 * W), BF16),
            pltpu.VMEM((CH, 3 * W), BF16),
            pltpu.VMEM((8, 2, 2, BS, W), F32),
            pltpu.VMEM((8, 2, BS, W), F32),
            pltpu.VMEM((8, 2, BS, W), BF16),
            pltpu.VMEM((16, BS, W), BF16),
            dma((2,)),
            dma((nch,)), dma((nch,)), dma((nch,)), dma((nch,)), dma((nch,)), dma((nch,)),
            dma((6,)), dma((6,)), dma((8,)), dma((8,)), dma((8, 2)), dma((16,)),
        ],
        compiler_params=pltpu.CompilerParams(
            collective_id=0, has_side_effects=True, vmem_limit_bytes=60 * 2**20
        ),
    )(modes, stiffness, offsets)
    return res.T


def solution(mesh):
    in_specs = (P("slab", "blk"), P("slab", None), P("slab", None))
    return jax.shard_map(body, mesh=mesh, in_specs=in_specs, out_specs=P("blk", "slab"), check_vma=False)
```

time: 568 us -> 143 us (0.25)
  the two profiles are of different devices: /device:TPU:19 before, /device:TPU:103 now
where the time goes in v1:
time: 143 us
  Pallas kernels  140 us (98%)
  local copies, waits for them, and re-layouts  2.86 us (2%)
    pallas_call x1, Pallas kernels, body(): pl.pallas_call(kernel, out_shape=jax.ShapeDtypeStruct((BS, W), F32), in_s...  140 us

profile of v1, /device:TPU:103, one launch (start us, length us, event | category | flops | bytes accessed | tf_op | source)
XLA Modules:
  0.0 143.1 jit_solution(11713219161137715184)
XLA Ops:
  0.0 1.4 copy.4.offs
  1.4 140.3 %shard_map.37 = f32[64,256]{1,0:T(8,128)} custom-call(bf16[4096,256]{1,0:T(8,128)(2,1)} %modes.1, bf16[4096,512]{1,0:T(8,128)(2,1)} %stiff.1, s32[64,8]{1,0:T(8,128)} %copy.4.offs), custom_call_target="tpu_custom_call" | custom-call | tf_op jit(solution)/shard_map/pallas_call | solution.py:254
  141.7 1.5 %copy.6 = f32[256,64]{0,1:T(8,128)} copy(f32[256,64]{0,1:T(8,128)} %bitcast.1) | data formatting | bytes 131072

commit v2 on v1

v2 whole, which is shorter than its diff:
```python
import jax
import jax.numpy as jnp
from jax import lax
from jax.experimental import pallas as pl
from jax.experimental.pallas import tpu as pltpu
from jax.sharding import PartitionSpec as P

MESH = pl.DeviceIdType.MESH
BS = 64
CH = 256
BPC = CH // BS
W = 256
F32 = jnp.float32
BF16 = jnp.bfloat16

O, U, D, Q = (0, 0), (0, 1), (0, 3), (1, 3)
PAIRS = ((O, O), (O, Q), (U, O), (U, Q), (D, O), (D, Q), (D, U), (Q, O))
SHIFT = (0, 2, 7, 3, 5, 4, 1, 6)
ORDER = (5, 3, 4, 1, 7, 2, 6, 0)
AHEAD = 3


def kernel(
    modes, stiff, offs, out,
    own, kv, up, dn, qp, halo, hmid, ring, kphi, acc, xr, sb, fr, fin,
    lsem, yu_s, yu_r, yd_s, yd_r, xq_s, xq_r, h_s, h_r, c_s, c_r, f_s, f_r, e_s, e_r,
):
    s, b = lax.axis_index("slab"), lax.axis_index("blk")
    z, xl, core = s // 4, (s // 2) % 2, s % 2
    xh, y = b // 4, b % 4
    nch = modes.shape[0] // CH
    slabs = lax.axis_size("slab")

    def blk_at(d):
        return ((xh + d[0]) % 2) * 4 + (y + d[1]) % 4

    outer = lax.rem(s + 2 * core - 1 + slabs, slabs)
    inner = s + 1 - 2 * core
    y_up, y_dn, x_far = (s, blk_at((0, 1))), (s, blk_at((0, 3))), (s, blk_at((1, 0)))
    across, beyond = (inner, b), (outer, b)

    def chunk(t):
        return t * core + (nch - 1 - t) * (1 - core)

    def rows(t):
        return pl.ds(pl.multiple_of(chunk(t) * CH, CH), CH)

    way = 2 * core - 1

    aside = (outer, blk_at((1, 0)))

    def pick(hit, values):
        return sum(jnp.where(hit(p), values(p), 0) for p in range(8))

    def added(p):
        return (b + SHIFT[p]) % 8 == z

    goal = (
        pick(added, lambda p: blk_at(PAIRS[p][1])) * 4 + xl * 2 + core,
        pick(added, lambda p: blk_at(PAIRS[p][0])),
    )

    def wanted(p):
        r, c = PAIRS[p]
        dx, dy = (c[0] - r[0]) % 2, (c[1] - r[1]) % 4
        return ((xh + dx) % 2) * 4 + (y + dy) % 4 == z

    def site(p):
        r, _ = PAIRS[p]
        return blk_at(((-r[0]) % 2, (-r[1]) % 4))

    origin = (
        pick(wanted, lambda p: (site(p) + SHIFT[p]) % 8) * 4 + xl * 2 + core,
        pick(wanted, site),
    )
    mine = z * 2 + xl
    moves = (z != b).astype(jnp.int32)

    copy_k = pltpu.make_async_copy(stiff, kv, lsem.at[0])
    copy_o = pltpu.make_async_copy(modes, own, lsem.at[1])
    copy_k.start()
    copy_o.start()

    barrier = pltpu.get_barrier_semaphore()
    for dev in (y_up, y_dn, x_far, across, beyond, aside):
        pl.semaphore_signal(barrier, inc=1, device_id=dev, device_id_type=MESH)

    @pl.loop(0, 16)
    def _(i):
        @pl.when(i != mine)
        def _():
            pl.semaphore_signal(barrier, inc=1, device_id=(i * 2 + core, b), device_id_type=MESH)

    @pl.when(moves > 0)
    def _():
        pl.semaphore_signal(barrier, inc=1, device_id=origin, device_id_type=MESH)

    pl.semaphore_wait(barrier, 6 + 15 + moves)

    def remote(src, dst, ssem, rsem, dev):
        return pltpu.make_async_remote_copy(src, dst, ssem, rsem, device_id=dev, device_id_type=MESH)

    def send_u(t):
        return remote(modes.at[rows(t)], up.at[rows(t)], yu_s.at[t], yu_r.at[t], y_dn)

    def send_d(t):
        return remote(modes.at[rows(t)], dn.at[rows(t)], yd_s.at[t], yd_r.at[t], y_up)

    def send_q(t):
        return remote(dn.at[rows(t)], qp.at[rows(t)], xq_s.at[t], xq_r.at[t], x_far)

    ho_out = remote(modes.at[rows(nch - 1)], halo.at[0, 1], h_s.at[0], h_r.at[0], beyond)
    ho_in = remote(modes.at[rows(0)], halo.at[0, 0], h_s.at[1], h_r.at[1], across)
    hu_out = remote(halo.at[0, 1], halo.at[2, 1], h_s.at[2], h_r.at[2], y_dn)
    hu_in = remote(up.at[rows(0)], halo.at[2, 0], h_s.at[3], h_r.at[3], across)
    hq_out = remote(hmid, halo.at[1, 1], h_s.at[4], h_r.at[4], y_up)
    hq_in = remote(qp.at[rows(0)], halo.at[1, 0], h_s.at[5], h_r.at[5], across)

    hx_out = remote(modes.at[rows(nch - 1)], hmid, h_s.at[6], h_r.at[6], aside)

    ho_out.start()
    hx_out.start()
    ho_in.start()

    @pl.loop(0, AHEAD)
    def _(t):
        send_u(t).start()
        send_d(t).start()

    acc[...] = jnp.zeros_like(acc)
    copy_k.wait()
    copy_o.wait()

    def fill(slot, parts):
        for p, part in enumerate(parts):
            ring[pl.ds(slot * BPC, BPC), :, p * W:(p + 1) * W] = part.reshape(BPC, BS, W)

    def compute(j):
        c = chunk(j)
        for i in range(BPC):
            line = c * BPC + i
            where = []
            for col in range(8):
                pos = offs[col, line] + i
                slot = (j + 1 + way * (pos >> 2)) & 3
                where.append(slot * BPC + (pos & 3))
            lhs = kv[pl.ds(pl.multiple_of(line * BS, BS), BS), :]
            for p in range(3):
                gathered = jnp.concatenate([ring[w, :, p * W:(p + 1) * W] for w in where], axis=0)
                kphi[i * BS:(i + 1) * BS, p * W:(p + 1) * W] = jnp.dot(
                    lhs, gathered, preferred_element_type=F32
                ).astype(BF16)
        first = 0
        for ref, n in ((own, 2), (up, 2), (dn, 3), (qp, 1)):
            prod = lax.dot_general(
                kphi[:, : n * W], ref[rows(j), :], (((0,), (0,)), ((), ())), preferred_element_type=F32
            )
            acc[first:first + n] += prod.reshape(n, 2, 2, BS, W)
            first += n

    lag = 2

    @pl.loop(0, nch + lag + 1)
    def _(t):
        @pl.when(t < nch)
        def _():
            send_d(t).wait_recv()
            send_q(t).start()

        @pl.when(t + AHEAD < nch)
        def _():
            send_u(t + AHEAD).start()
            send_d(t + AHEAD).start()

        @pl.when(t + AHEAD == nch)
        def _():
            ho_out.wait_recv()
            hu_out.start()
            hx_out.wait_recv()
            hq_out.start()

        j = t - lag

        @pl.when(j == 0)
        def _():
            send_u(0).wait_recv()
            hu_in.start()
            send_q(0).wait_recv()
            hq_in.start()
            hu_in.wait_recv()
            ho_in.wait_recv()
            hq_in.wait_recv()
            fill(0, (halo[0, 0], halo[1, 0], halo[2, 0]))

        @pl.when(jnp.logical_and(j >= 0, j < nch))
        def _():
            @pl.when(j > 0)
            def _():
                send_u(j).wait_recv()
                send_q(j).wait_recv()

            fill((j + 1) & 3, (own[rows(j), :], qp[rows(j), :], up[rows(j), :]))

        @pl.when(j == nch)
        def _():
            hu_out.wait_recv()
            hq_out.wait_recv()
            inside = jnp.logical_and(s + core > 0, s + core < slabs).astype(F32)
            fill(
                (nch + 1) & 3,
                [jnp.where(inside > 0, halo[p, 1], jnp.zeros((CH, W), BF16)) for p in range(3)],
            )

        @pl.when(j >= 1)
        def _():
            compute(j - 1)

    def swap(p):
        return remote(acc.at[p, :, 1 - core], xr.at[p], c_s.at[p], c_r.at[p], across)

    for p in ORDER:
        swap(p).start()

    def final(p, h):
        to = (b + SHIFT[p]) % 8
        dev = (to * 4 + h * 2 + core, b)
        return remote(sb.at[p, h], fr.at[mine], f_s.at[p, h], f_r.at[mine], dev), jnp.logical_and(to == z, h == xl)

    for p in ORDER:
        swap(p).wait_recv()
        sb[p] = (acc[p, :, core] + xr[p]).astype(BF16)
        for h in range(2):
            cp, stays = final(p, h)

            @pl.when(stays)
            def _():
                fr[mine] = sb[p, h]

            @pl.when(jnp.logical_not(stays))
            def _():
                cp.start()

    fin[0] = jnp.zeros((BS, W), F32)

    @pl.loop(0, 16)
    def _(i):
        @pl.when(i != mine)
        def _():
            remote(sb.at[0, 0], fr.at[i], f_s.at[0, 0], f_r.at[i], across).wait_recv()

        fin[0] += fr[i].astype(F32)

    home = remote(fin.at[0], fin.at[1], e_s, e_r, goal)

    @pl.when(moves > 0)
    def _():
        home.start()
        home.wait()
        out[...] = fin[1]

    @pl.when(moves == 0)
    def _():
        out[...] = fin[0]

    for cp in (ho_out, ho_in, hu_out, hu_in, hq_out, hq_in, hx_out):
        cp.wait_send()

    @pl.loop(0, nch)
    def _(t):
        send_u(t).wait_send()
        send_d(t).wait_send()
        send_q(t).wait_send()

    for p in range(8):
        swap(p).wait_send()
        for h in range(2):
            cp, stays = final(p, h)

            @pl.when(jnp.logical_not(stays))
            def _():
                cp.wait_send()


def body(modes, stiffness, offsets):
    n, w = modes.shape
    nch = n // CH
    dma = pltpu.SemaphoreType.DMA
    res = pl.pallas_call(
        kernel,
        out_shape=jax.ShapeDtypeStruct((BS, W), F32),
        in_specs=[
            pl.BlockSpec(memory_space=pl.ANY),
            pl.BlockSpec(memory_space=pl.ANY),
            pl.BlockSpec(memory_space=pltpu.SMEM),
        ],
        out_specs=pl.BlockSpec(memory_space=pltpu.VMEM),
        scratch_shapes=[
            pltpu.VMEM((n, w), BF16),
            pltpu.VMEM((n, 8 * BS), BF16),
            pltpu.VMEM((n, w), BF16),
            pltpu.VMEM((n, w), BF16),
            pltpu.VMEM((n, w), BF16),
            pltpu.VMEM((3, 2, CH, w), BF16),
            pltpu.VMEM((CH, w), BF16),
            pltpu.VMEM((4 * BPC, BS, 3 * W), BF16),
            pltpu.VMEM((CH, 3 * W), BF16),
            pltpu.VMEM((8, 2, 2, BS, W), F32),
            pltpu.VMEM((8, 2, BS, W), F32),
            pltpu.VMEM((8, 2, BS, W), BF16),
            pltpu.VMEM((16, BS, W), BF16),
            pltpu.VMEM((2, BS, W), F32),
            dma((2,)),
            dma((nch,)), dma((nch,)), dma((nch,)), dma((nch,)), dma((nch,)), dma((nch,)),
            dma((7,)), dma((7,)), dma((8,)), dma((8,)), dma((8, 2)), dma((16,)), dma, dma,
        ],
        compiler_params=pltpu.CompilerParams(
            collective_id=0, has_side_effects=True, vmem_limit_bytes=60 * 2**20
        ),
    )(modes, stiffness, offsets.T)
    return res.T


def solution(mesh):
    in_specs = (P("slab", "blk"), P("slab", None), P("slab", None))
    return jax.shard_map(body, mesh=mesh, in_specs=in_specs, out_specs=P("blk", "slab"), check_vma=False)
```

time: 143 us -> 91.8 us (0.64)
  the two profiles are of different devices: /device:TPU:103 before, /device:TPU:10 now
where the time goes in v2:
time: 91.8 us; the launch traced here: 91.6 us
  Pallas kernels  90.2 us (98%)
  local copies, waits for them, and re-layouts  1.47 us (2%)
    pallas_call x1, Pallas kernels, body(): pl.pallas_call(kernel, out_shape=jax.ShapeDtypeStruct((BS, W), F32), in_s...  90.2 us

profile of v2, /device:TPU:10, one launch (start us, length us, event | category | flops | bytes accessed | tf_op | source)
XLA Modules:
  0.0 91.6 jit_solution(1829270455325193661)
XLA Ops:
  0.0 90.2 %shard_map.37 = f32[64,256]{1,0:T(8,128)} custom-call(bf16[4096,256]{1,0:T(8,128)(2,1)} %modes.1, bf16[4096,512]{1,0:T(8,128)(2,1)} %stiff.1, s32[8,64]{1,0:T(8,128)} %bitcast.3), custom_call_target="tpu_custom_call" | custom-call | tf_op jit(solution)/shard_map/pallas_call | solution.py:288
  90.2 1.5 %copy.5 = f32[256,64]{0,1:T(8,128)} copy(f32[256,64]{0,1:T(8,128)} %bitcast.2) | data formatting | bytes 131072

commit v3 on v2

--- a/solution.py
+++ b/solution.py
@@ -15,15 +15,14 @@
 
 O, U, D, Q = (0, 0), (0, 1), (0, 3), (1, 3)
 PAIRS = ((O, O), (O, Q), (U, O), (U, Q), (D, O), (D, Q), (D, U), (Q, O))
-SHIFT = (0, 2, 7, 3, 5, 4, 1, 6)
-ORDER = (5, 3, 4, 1, 7, 2, 6, 0)
+ORDER = (0, 4, 2, 7, 1, 5, 3, 6)
 AHEAD = 3
 
 
 def kernel(
     modes, stiff, offs, out,
-    own, kv, up, dn, qp, halo, hmid, ring, kphi, acc, xr, sb, fr, fin,
-    lsem, yu_s, yu_r, yd_s, yd_r, xq_s, xq_r, h_s, h_r, c_s, c_r, f_s, f_r, e_s, e_r,
+    own, kv, up, dn, qp, halo, hmid, ring, kphi, acc, xr, sb, mid, fr,
+    lsem, yu_s, yu_r, yd_s, yd_r, xq_s, xq_r, h_s, h_r, c_s, c_r, f_s, f_r, m_s, m_r, tok,
 ):
     s, b = lax.axis_index("slab"), lax.axis_index("blk")
     z, xl, core = s // 4, (s // 2) % 2, s % 2
@@ -49,32 +48,9 @@
 
     aside = (outer, blk_at((1, 0)))
 
-    def pick(hit, values):
-        return sum(jnp.where(hit(p), values(p), 0) for p in range(8))
-
-    def added(p):
-        return (b + SHIFT[p]) % 8 == z
-
-    goal = (
-        pick(added, lambda p: blk_at(PAIRS[p][1])) * 4 + xl * 2 + core,
-        pick(added, lambda p: blk_at(PAIRS[p][0])),
-    )
-
-    def wanted(p):
-        r, c = PAIRS[p]
-        dx, dy = (c[0] - r[0]) % 2, (c[1] - r[1]) % 4
-        return ((xh + dx) % 2) * 4 + (y + dy) % 4 == z
-
-    def site(p):
-        r, _ = PAIRS[p]
-        return blk_at(((-r[0]) % 2, (-r[1]) % 4))
-
-    origin = (
-        pick(wanted, lambda p: (site(p) + SHIFT[p]) % 8) * 4 + xl * 2 + core,
-        pick(wanted, site),
-    )
+    z_up, z_dn = (lax.rem(s + 4, slabs), b), (lax.rem(s + slabs - 4, slabs), b)
+    beside = (s + 2 - 4 * xl, b)
     mine = z * 2 + xl
-    moves = (z != b).astype(jnp.int32)
 
     copy_k = pltpu.make_async_copy(stiff, kv, lsem.at[0])
     copy_o = pltpu.make_async_copy(modes, own, lsem.at[1])
@@ -82,20 +58,24 @@
     copy_o.start()
 
     barrier = pltpu.get_barrier_semaphore()
-    for dev in (y_up, y_dn, x_far, across, beyond, aside):
+    near = (y_up, y_dn, x_far, across, beyond, aside, (s, blk_at((1, 1))), z_up, z_dn, beside)
+    for dev in near:
         pl.semaphore_signal(barrier, inc=1, device_id=dev, device_id_type=MESH)
-
-    @pl.loop(0, 16)
-    def _(i):
-        @pl.when(i != mine)
-        def _():
-            pl.semaphore_signal(barrier, inc=1, device_id=(i * 2 + core, b), device_id_type=MESH)
-
-    @pl.when(moves > 0)
-    def _():
-        pl.semaphore_signal(barrier, inc=1, device_id=origin, device_id_type=MESH)
-
-    pl.semaphore_wait(barrier, 6 + 15 + moves)
+    pl.semaphore_wait(barrier, len(near))
+
+    def tell(k):
+        if k < 3:
+            pl.semaphore_signal(tok.at[2 * k], inc=1, device_id=z_up, device_id_type=MESH)
+            pl.semaphore_signal(tok.at[2 * k + 1], inc=1, device_id=z_dn, device_id_type=MESH)
+        else:
+            pl.semaphore_signal(tok.at[6], inc=1, device_id=beside, device_id_type=MESH)
+
+    def hear(k):
+        if k < 3:
+            pl.semaphore_wait(tok.at[2 * k], 1)
+            pl.semaphore_wait(tok.at[2 * k + 1], 1)
+        else:
+            pl.semaphore_wait(tok.at[6], 1)
 
     def remote(src, dst, ssem, rsem, dev):
         return pltpu.make_async_remote_copy(src, dst, ssem, rsem, device_id=dev, device_id_type=MESH)
@@ -179,6 +159,14 @@
             hx_out.wait_recv()
             hq_out.start()
 
+        for k in range(5):
+            @pl.when(t == 2 * k + 2)
+            def _():
+                if k > 0:
+                    hear(k - 1)
+                if k < 4:
+                    tell(k)
+
         j = t - lag
 
         @pl.when(j == 0)
@@ -222,25 +210,40 @@
         swap(p).start()
 
     def final(p, h):
-        to = (b + SHIFT[p]) % 8
-        dev = (to * 4 + h * 2 + core, b)
-        return remote(sb.at[p, h], fr.at[mine], f_s.at[p, h], f_r.at[mine], dev), jnp.logical_and(to == z, h == xl)
+        r, c = PAIRS[p]
+        to = blk_at(((c[0] - r[0]) % 2, (c[1] - r[1]) % 4))
+        piece = sb.at[p, h] if r == O else mid.at[p, h]
+        cp = remote(piece, fr.at[mine], f_s.at[p, h], f_r.at[mine], (to * 4 + h * 2 + core, b))
+        return cp, piece, jnp.logical_and(to == z, h == xl)
+
+    def move(p):
+        return remote(sb.at[p], mid.at[p], m_s.at[p], m_r.at[p], (s, blk_at(PAIRS[p][0])))
+
+    def settle(p):
+        for h in range(2):
+            cp, piece, stays = final(p, h)
+
+            @pl.when(stays)
+            def _():
+                fr[mine] = piece[...]
+
+            @pl.when(jnp.logical_not(stays))
+            def _():
+                cp.start()
 
     for p in ORDER:
         swap(p).wait_recv()
         sb[p] = (acc[p, :, core] + xr[p]).astype(BF16)
-        for h in range(2):
-            cp, stays = final(p, h)
-
-            @pl.when(stays)
-            def _():
-                fr[mine] = sb[p, h]
-
-            @pl.when(jnp.logical_not(stays))
-            def _():
-                cp.start()
-
-    fin[0] = jnp.zeros((BS, W), F32)
+        if PAIRS[p][0] == O:
+            settle(p)
+        else:
+            move(p).start()
+    for p in ORDER:
+        if PAIRS[p][0] != O:
+            move(p).wait_recv()
+            settle(p)
+
+    out[...] = jnp.zeros((BS, W), F32)
 
     @pl.loop(0, 16)
     def _(i):
@@ -248,19 +251,7 @@
         def _():
             remote(sb.at[0, 0], fr.at[i], f_s.at[0, 0], f_r.at[i], across).wait_recv()
 
-        fin[0] += fr[i].astype(F32)
-
-    home = remote(fin.at[0], fin.at[1], e_s, e_r, goal)
-
-    @pl.when(moves > 0)
-    def _():
-        home.start()
-        home.wait()
-        out[...] = fin[1]
-
-    @pl.when(moves == 0)
-    def _():
-        out[...] = fin[0]
+        out[...] += fr[i].astype(F32)
 
     for cp in (ho_out, ho_in, hu_out, hu_in, hq_out, hq_in, hx_out):
         cp.wait_send()
@@ -273,8 +264,10 @@
 
     for p in range(8):
         swap(p).wait_send()
+        if PAIRS[p][0] != O:
+            move(p).wait_send()
         for h in range(2):
-            cp, stays = final(p, h)
+            cp, _, stays = final(p, h)
 
             @pl.when(jnp.logical_not(stays))
             def _():
@@ -307,11 +300,12 @@
             pltpu.VMEM((8, 2, 2, BS, W), F32),
             pltpu.VMEM((8, 2, BS, W), F32),
             pltpu.VMEM((8, 2, BS, W), BF16),
+            pltpu.VMEM((8, 2, BS, W), BF16),
             pltpu.VMEM((16, BS, W), BF16),
-            pltpu.VMEM((2, BS, W), F32),
             dma((2,)),
             dma((nch,)), dma((nch,)), dma((nch,)), dma((nch,)), dma((nch,)), dma((nch,)),
-            dma((7,)), dma((7,)), dma((8,)), dma((8,)), dma((8, 2)), dma((16,)), dma, dma,
+            dma((7,)), dma((7,)), dma((8,)), dma((8,)), dma((8, 2)), dma((16,)), dma((8,)), dma((8,)),
+            pltpu.SemaphoreType.REGULAR((7,)),
         ],
         compiler_params=pltpu.CompilerParams(
             collective_id=0, has_side_effects=True, vmem_limit_bytes=60 * 2**20

time: 91.8 us -> 88 us (0.959)
  the two profiles are of different devices: /device:TPU:10 before, /device:TPU:19 now
where the time goes in v3:
time: 88 us; the launch traced here: 87.8 us
  Pallas kernels  86.4 us (98%)
  local copies, waits for them, and re-layouts  1.47 us (2%)
    pallas_call x1, Pallas kernels, body(): pl.pallas_call(kernel, out_shape=jax.ShapeDtypeStruct((BS, W), F32), in_s...  86.4 us

profile of v3, /device:TPU:19, one launch (start us, length us, event | category | flops | bytes accessed | tf_op | source)
XLA Modules:
  0.0 87.8 jit_solution(13476092532862748400)
XLA Ops:
  0.0 86.4 %shard_map.37 = f32[64,256]{1,0:T(8,128)} custom-call(bf16[4096,256]{1,0:T(8,128)(2,1)} %modes.1, bf16[4096,512]{1,0:T(8,128)(2,1)} %stiff.1, s32[8,64]{1,0:T(8,128)} %bitcast.3), custom_call_target="tpu_custom_call" | custom-call | tf_op jit(solution)/shard_map/pallas_call | solution.py:281
  86.4 1.5 %copy.5 = f32[256,64]{0,1:T(8,128)} copy(f32[256,64]{0,1:T(8,128)} %bitcast.2) | data formatting | bytes 131072

commit v4 on v3

--- a/solution.py
+++ b/solution.py
@@ -15,13 +15,17 @@
 
 O, U, D, Q = (0, 0), (0, 1), (0, 3), (1, 3)
 PAIRS = ((O, O), (O, Q), (U, O), (U, Q), (D, O), (D, Q), (D, U), (Q, O))
-ORDER = (0, 4, 2, 7, 1, 5, 3, 6)
+EARLY = (2, 4, 0)
+STEPS = (
+    (2, True), (4, True), (7, False), (5, False), (3, False), (6, False), (1, False),
+    (7, True), (5, True), (3, True), (6, True),
+)
 AHEAD = 3
 
 
 def kernel(
-    modes, stiff, offs, out,
-    own, kv, up, dn, qp, halo, hmid, ring, kphi, acc, xr, sb, mid, fr,
+    modes, stiff, offsets, out,
+    offs, own, kv, up, dn, qp, halo, hmid, ring_o, ring, kphi_o, kphi, acc, xr, sb, mid, fr,
     lsem, yu_s, yu_r, yd_s, yd_r, xq_s, xq_r, h_s, h_r, c_s, c_r, f_s, f_r, m_s, m_r, tok,
 ):
     s, b = lax.axis_index("slab"), lax.axis_index("blk")
@@ -54,6 +58,8 @@
 
     copy_k = pltpu.make_async_copy(stiff, kv, lsem.at[0])
     copy_o = pltpu.make_async_copy(modes, own, lsem.at[1])
+    copy_f = pltpu.make_async_copy(offsets, offs, lsem.at[2])
+    copy_f.start()
     copy_k.start()
     copy_o.start()
 
@@ -108,14 +114,15 @@
         send_d(t).start()
 
     acc[...] = jnp.zeros_like(acc)
+    copy_f.wait()
     copy_k.wait()
     copy_o.wait()
 
-    def fill(slot, parts):
+    def fill(ref, slot, parts):
         for p, part in enumerate(parts):
-            ring[pl.ds(slot * BPC, BPC), :, p * W:(p + 1) * W] = part.reshape(BPC, BS, W)
-
-    def compute(j):
+            ref[pl.ds(slot * BPC, BPC), :, p * W:(p + 1) * W] = part.reshape(BPC, BS, W)
+
+    def stage1(j, ref, panels, store):
         c = chunk(j)
         for i in range(BPC):
             line = c * BPC + i
@@ -125,89 +132,44 @@
                 slot = (j + 1 + way * (pos >> 2)) & 3
                 where.append(slot * BPC + (pos & 3))
             lhs = kv[pl.ds(pl.multiple_of(line * BS, BS), BS), :]
-            for p in range(3):
-                gathered = jnp.concatenate([ring[w, :, p * W:(p + 1) * W] for w in where], axis=0)
-                kphi[i * BS:(i + 1) * BS, p * W:(p + 1) * W] = jnp.dot(
-                    lhs, gathered, preferred_element_type=F32
-                ).astype(BF16)
-        first = 0
-        for ref, n in ((own, 2), (up, 2), (dn, 3), (qp, 1)):
-            prod = lax.dot_general(
-                kphi[:, : n * W], ref[rows(j), :], (((0,), (0,)), ((), ())), preferred_element_type=F32
-            )
-            acc[first:first + n] += prod.reshape(n, 2, 2, BS, W)
-            first += n
-
-    lag = 2
-
-    @pl.loop(0, nch + lag + 1)
-    def _(t):
-        @pl.when(t < nch)
-        def _():
-            send_d(t).wait_recv()
-            send_q(t).start()
-
-        @pl.when(t + AHEAD < nch)
-        def _():
-            send_u(t + AHEAD).start()
-            send_d(t + AHEAD).start()
-
-        @pl.when(t + AHEAD == nch)
-        def _():
-            ho_out.wait_recv()
-            hu_out.start()
-            hx_out.wait_recv()
-            hq_out.start()
-
-        for k in range(5):
-            @pl.when(t == 2 * k + 2)
-            def _():
-                if k > 0:
-                    hear(k - 1)
-                if k < 4:
-                    tell(k)
-
-        j = t - lag
-
-        @pl.when(j == 0)
-        def _():
-            send_u(0).wait_recv()
-            hu_in.start()
-            send_q(0).wait_recv()
-            hq_in.start()
-            hu_in.wait_recv()
-            ho_in.wait_recv()
-            hq_in.wait_recv()
-            fill(0, (halo[0, 0], halo[1, 0], halo[2, 0]))
-
-        @pl.when(jnp.logical_and(j >= 0, j < nch))
-        def _():
-            @pl.when(j > 0)
-            def _():
-                send_u(j).wait_recv()
-                send_q(j).wait_recv()
-
-            fill((j + 1) & 3, (own[rows(j), :], qp[rows(j), :], up[rows(j), :]))
-
-        @pl.when(j == nch)
-        def _():
-            hu_out.wait_recv()
-            hq_out.wait_recv()
-            inside = jnp.logical_and(s + core > 0, s + core < slabs).astype(F32)
-            fill(
-                (nch + 1) & 3,
-                [jnp.where(inside > 0, halo[p, 1], jnp.zeros((CH, W), BF16)) for p in range(3)],
-            )
-
-        @pl.when(j >= 1)
-        def _():
-            compute(j - 1)
+            for p in range(panels):
+                gathered = jnp.concatenate([ref[w, :, p * W:(p + 1) * W] for w in where], axis=0)
+                store(i, p, jnp.dot(lhs, gathered, preferred_element_type=F32).astype(BF16))
+
+    def add(first, n, left, right):
+        prod = lax.dot_general(left, right, (((0,), (0,)), ((), ())), preferred_element_type=F32)
+        acc[first:first + n] += prod.reshape(n, 2, 2, BS, W)
+
+    def early(j):
+        base = chunk(j) * CH
+
+        def store(i, p, value):
+            kphi_o[pl.ds(pl.multiple_of(base + i * BS, BS), BS), :] = value
+
+        stage1(j, ring_o, 1, store)
+        for ref, p in ((up, 2), (dn, 4), (own, 0)):
+            add(p, 1, kphi_o[rows(j), :], ref[rows(j), :])
+
+    def late(j, done=None):
+        def store(i, p, value):
+            kphi[i * BS:(i + 1) * BS, p * W:(p + 1) * W] = value
+
+        stage1(j, ring, 2, store)
+        for first, n, left, right in (
+            (7, 1, kphi_o[rows(j), :], qp), (5, 2, kphi[...], dn), (3, 1, kphi[:, :W], up), (1, 1, kphi[:, :W], own),
+        ):
+            add(first, n, left, right[rows(j), :])
+            for p in range(first, first + n):
+                if done is not None:
+                    done(p)
+
+    inside = jnp.logical_and(s + core > 0, s + core < slabs).astype(F32)
+
+    def beyond_face(p):
+        return jnp.where(inside > 0, halo[p, 1], jnp.zeros((CH, W), BF16))
 
     def swap(p):
         return remote(acc.at[p, :, 1 - core], xr.at[p], c_s.at[p], c_r.at[p], across)
-
-    for p in ORDER:
-        swap(p).start()
 
     def final(p, h):
         r, c = PAIRS[p]
@@ -231,17 +193,105 @@
             def _():
                 cp.start()
 
-    for p in ORDER:
+    def leave(p):
         swap(p).wait_recv()
         sb[p] = (acc[p, :, core] + xr[p]).astype(BF16)
         if PAIRS[p][0] == O:
             settle(p)
         else:
             move(p).start()
-    for p in ORDER:
-        if PAIRS[p][0] != O:
+
+    lag = 2
+
+    @pl.loop(0, nch + lag)
+    def _(t):
+        @pl.when(t < nch)
+        def _():
+            send_d(t).wait_recv()
+            send_q(t).start()
+
+        @pl.when(t + AHEAD < nch)
+        def _():
+            send_u(t + AHEAD).start()
+            send_d(t + AHEAD).start()
+
+        @pl.when(t + AHEAD == nch)
+        def _():
+            ho_out.wait_recv()
+            hu_out.start()
+            hx_out.wait_recv()
+            hq_out.start()
+
+        for k in range(5):
+            @pl.when(t == 2 * k + 2)
+            def _():
+                if k > 0:
+                    hear(k - 1)
+                if k < 4:
+                    tell(k)
+
+        @pl.when(t == 0)
+        def _():
+            ho_in.wait_recv()
+            fill(ring_o, 0, (halo[0, 0],))
+
+        @pl.when(t < nch)
+        def _():
+            fill(ring_o, (t + 1) & 3, (own[rows(t), :],))
+
+        @pl.when(t == nch)
+        def _():
+            fill(ring_o, (nch + 1) & 3, (beyond_face(0),))
+
+        @pl.when(jnp.logical_and(t >= 1, t <= nch))
+        def _():
+            send_u(t - 1).wait_recv()
+            early(t - 1)
+
+        @pl.when(t == nch)
+        def _():
+            for p in EARLY:
+                swap(p).start()
+
+        @pl.when(t == nch + 1)
+        def _():
+            for p in EARLY:
+                leave(p)
+
+        j = t - lag
+
+        @pl.when(j == 0)
+        def _():
+            hu_in.start()
+            send_q(0).wait_recv()
+            hq_in.start()
+            hu_in.wait_recv()
+            hq_in.wait_recv()
+            fill(ring, 0, (halo[1, 0], halo[2, 0]))
+
+        @pl.when(j >= 0)
+        def _():
+            @pl.when(j > 0)
+            def _():
+                send_q(j).wait_recv()
+
+            fill(ring, (j + 1) & 3, (qp[rows(j), :], up[rows(j), :]))
+
+        @pl.when(j >= 1)
+        def _():
+            late(j - 1)
+
+    hu_out.wait_recv()
+    hq_out.wait_recv()
+    fill(ring, (nch + 1) & 3, (beyond_face(1), beyond_face(2)))
+    late(nch - 1, lambda p: swap(p).start())
+
+    for p, arrived in STEPS:
+        if arrived:
             move(p).wait_recv()
             settle(p)
+        else:
+            leave(p)
 
     out[...] = jnp.zeros((BS, W), F32)
 
@@ -284,10 +334,11 @@
         in_specs=[
             pl.BlockSpec(memory_space=pl.ANY),
             pl.BlockSpec(memory_space=pl.ANY),
-            pl.BlockSpec(memory_space=pltpu.SMEM),
+            pl.BlockSpec(memory_space=pl.ANY),
         ],
         out_specs=pl.BlockSpec(memory_space=pltpu.VMEM),
         scratch_shapes=[
+            pltpu.SMEM(offsets.shape[::-1], jnp.int32),
             pltpu.VMEM((n, w), BF16),
             pltpu.VMEM((n, 8 * BS), BF16),
             pltpu.VMEM((n, w), BF16),
@@ -295,14 +346,16 @@
             pltpu.VMEM((n, w), BF16),
             pltpu.VMEM((3, 2, CH, w), BF16),
             pltpu.VMEM((CH, w), BF16),
-            pltpu.VMEM((4 * BPC, BS, 3 * W), BF16),
-            pltpu.VMEM((CH, 3 * W), BF16),
+            pltpu.VMEM((4 * BPC, BS, W), BF16),
+            pltpu.VMEM((4 * BPC, BS, 2 * W), BF16),
+            pltpu.VMEM((n, W), BF16),
+            pltpu.VMEM((CH, 2 * W), BF16),
             pltpu.VMEM((8, 2, 2, BS, W), F32),
             pltpu.VMEM((8, 2, BS, W), F32),
             pltpu.VMEM((8, 2, BS, W), BF16),
             pltpu.VMEM((8, 2, BS, W), BF16),
             pltpu.VMEM((16, BS, W), BF16),
-            dma((2,)),
+            dma((3,)),
             dma((nch,)), dma((nch,)), dma((nch,)), dma((nch,)), dma((nch,)), dma((nch,)),
             dma((7,)), dma((7,)), dma((8,)), dma((8,)), dma((8, 2)), dma((16,)), dma((8,)), dma((8,)),
             pltpu.SemaphoreType.REGULAR((7,)),

time: 88 us -> 86 us (0.977); the launches traced: 87.8 us -> 84.6 us
  Pallas kernels: 86.4 us -> 83.1 us
    pallas_call x1, Pallas kernels: 86.4 us -> 83.1 us  [body(): pl.pallas_call(kernel, out_shape=jax.ShapeDtypeStruct((BS, W), F32), in_s...]
where the time goes in v4:
time: 86 us; the launch traced here: 84.6 us
  Pallas kernels  83.1 us (97%)
  local copies, waits for them, and re-layouts  1.47 us (2%)
    pallas_call x1, Pallas kernels, body(): pl.pallas_call(kernel, out_shape=jax.ShapeDtypeStruct((BS, W), F32), in_s...  83.1 us

profile of v4, /device:TPU:19, one launch (start us, length us, event | category | flops | bytes accessed | tf_op | source)
XLA Modules:
  0.0 84.6 jit_solution(16630276346744707832)
XLA Ops:
  0.0 83.1 %shard_map.37 = f32[64,256]{1,0:T(8,128)} custom-call(bf16[4096,256]{1,0:T(8,128)(2,1)} %modes.1, bf16[4096,512]{1,0:T(8,128)(2,1)} %stiff.1, s32[8,64]{1,0:T(8,128)} %bitcast.3), custom_call_target="tpu_custom_call" | custom-call | tf_op jit(solution)/shard_map/pallas_call | solution.py:331
  83.1 1.5 %copy.5 = f32[256,64]{0,1:T(8,128)} copy(f32[256,64]{0,1:T(8,128)} %bitcast.2) | data formatting | bytes 131072

commit v5 on v4

--- a/solution.py
+++ b/solution.py
@@ -14,11 +14,11 @@
 BF16 = jnp.bfloat16
 
 O, U, D, Q = (0, 0), (0, 1), (0, 3), (1, 3)
-PAIRS = ((O, O), (O, Q), (U, O), (U, Q), (D, O), (D, Q), (D, U), (Q, O))
-EARLY = (2, 4, 0)
+PAIRS = ((O, O), (O, Q), (O, U), (U, O), (U, Q), (D, Q), (D, U), (Q, O))
+EARLY = (3, 0)
 STEPS = (
-    (2, True), (4, True), (7, False), (5, False), (3, False), (6, False), (1, False),
-    (7, True), (5, True), (3, True), (6, True),
+    (3, True), (5, False), (4, False), (7, False), (6, False), (1, False), (2, False),
+    (5, True), (4, True), (7, True), (6, True),
 )
 AHEAD = 3
 
@@ -147,7 +147,7 @@
             kphi_o[pl.ds(pl.multiple_of(base + i * BS, BS), BS), :] = value
 
         stage1(j, ring_o, 1, store)
-        for ref, p in ((up, 2), (dn, 4), (own, 0)):
+        for ref, p in ((up, 3), (own, 0)):
             add(p, 1, kphi_o[rows(j), :], ref[rows(j), :])
 
     def late(j, done=None):
@@ -156,7 +156,7 @@
 
         stage1(j, ring, 2, store)
         for first, n, left, right in (
-            (7, 1, kphi_o[rows(j), :], qp), (5, 2, kphi[...], dn), (3, 1, kphi[:, :W], up), (1, 1, kphi[:, :W], own),
+            (5, 2, kphi[...], dn), (4, 1, kphi[:, :W], up), (7, 1, kphi_o[rows(j), :], qp), (1, 2, kphi[...], own),
         ):
             add(first, n, left, right[rows(j), :])
             for p in range(first, first + n):
@@ -253,11 +253,6 @@
             for p in EARLY:
                 swap(p).start()
 
-        @pl.when(t == nch + 1)
-        def _():
-            for p in EARLY:
-                leave(p)
-
         j = t - lag
 
         @pl.when(j == 0)
@@ -284,6 +279,8 @@
     hu_out.wait_recv()
     hq_out.wait_recv()
     fill(ring, (nch + 1) & 3, (beyond_face(1), beyond_face(2)))
+    for p in EARLY:
+        leave(p)
     late(nch - 1, lambda p: swap(p).start())
 
     for p, arrived in STEPS:

time: 86 us -> 85.3 us (level)
  Pallas kernels: 83.1 us -> 82.2 us
where the time goes in v5:
time: 85.3 us; the launch traced here: 83.7 us
  Pallas kernels  82.2 us (96%)
  local copies, waits for them, and re-layouts  1.47 us (2%)
    pallas_call x1, Pallas kernels, body(): pl.pallas_call(kernel, out_shape=jax.ShapeDtypeStruct((BS, W), F32), in_s...  82.2 us

profile of v5, /device:TPU:19, one launch (start us, length us, event | category | flops | bytes accessed | tf_op | source)
XLA Modules:
  0.0 83.7 jit_solution(7075484383087464085)
XLA Ops:
  0.0 82.2 %shard_map.37 = f32[64,256]{1,0:T(8,128)} custom-call(bf16[4096,256]{1,0:T(8,128)(2,1)} %modes.1, bf16[4096,512]{1,0:T(8,128)(2,1)} %stiff.1, s32[8,64]{1,0:T(8,128)} %bitcast.3), custom_call_target="tpu_custom_call" | custom-call | tf_op jit(solution)/shard_map/pallas_call | solution.py:328
  82.3 1.5 %copy.5 = f32[256,64]{0,1:T(8,128)} copy(f32[256,64]{0,1:T(8,128)} %bitcast.2) | data formatting | bytes 131072

commit v6 on v5

--- a/solution.py
+++ b/solution.py
@@ -17,8 +17,8 @@
 PAIRS = ((O, O), (O, Q), (O, U), (U, O), (U, Q), (D, Q), (D, U), (Q, O))
 EARLY = (3, 0)
 STEPS = (
-    (3, True), (5, False), (4, False), (7, False), (6, False), (1, False), (2, False),
-    (5, True), (4, True), (7, True), (6, True),
+    (5, False), (4, False), (6, False), (7, False), (1, False), (2, False),
+    (3, True), (5, True), (4, True), (6, True), (7, True),
 )
 AHEAD = 3
 

time: 85.3 us -> 86.4 us (1.013)
  the two profiles are of different devices: /device:TPU:19 before, /device:TPU:36 now
where the time goes in v6:
time: 86.4 us; the launch traced here: 86.3 us
  Pallas kernels  84.8 us (98%)
  local copies, waits for them, and re-layouts  1.47 us (2%)
    pallas_call x1, Pallas kernels, body(): pl.pallas_call(kernel, out_shape=jax.ShapeDtypeStruct((BS, W), F32), in_s...  84.8 us

profile of v6, /device:TPU:36, one launch (start us, length us, event | category | flops | bytes accessed | tf_op | source)
XLA Modules:
  0.0 86.3 jit_solution(7589977523281320971)
XLA Ops:
  0.0 84.8 %shard_map.37 = f32[64,256]{1,0:T(8,128)} custom-call(bf16[4096,256]{1,0:T(8,128)(2,1)} %modes.1, bf16[4096,512]{1,0:T(8,128)(2,1)} %stiff.1, s32[8,64]{1,0:T(8,128)} %bitcast.3), custom_call_target="tpu_custom_call" | custom-call | tf_op jit(solution)/shard_map/pallas_call | solution.py:328
  84.8 1.5 %copy.5 = f32[256,64]{0,1:T(8,128)} copy(f32[256,64]{0,1:T(8,128)} %bitcast.2) | data formatting | bytes 131072
